TPU v7x, 128 devices: a whole 4x4x4 slice. The times are simulated.
128 devices in a mesh: mode: 32 (over x, y, core), wall: 2 (over z_lo), ckpt: 2 (over z_hi).
Axes of the slice: x: 4, y: 4, z: 4 (z_hi: 2, z_lo: 2; z = z_hi * 2 + z_lo), core: 2. Of those that a mesh axis runs over, the one named last changes fastest.
Arguments:
- adjoint: float32 [2, 5, 1024, 4096], P(None, None, ('wall', 'ckpt'), 'mode'), may hold values from -6 to 6
- forward: float32 [2, 2, 1024, 4096], P('ckpt', None, 'wall', 'mode'), may hold values from -0.09375 to 0.09375
- mode_map: int32 [4096], P('mode'), may hold values from 0 to 4095, as said below
Outputs:
- adjoint_prev: float32 [2, 5, 1024, 4096], P(None, None, ('wall', 'ckpt'), 'mode')
Inputs may be any that keep to these rules, and one draw needn't show every extreme that they name: mode_map is a permutation of the 64 x 64 modes laid out by frequency: for every block b of 64 consecutive slots there is a frequency p(b) such that slot b * 64 + r holds mode p(b) * 64 + r, and p takes every frequency once.
All inputs are finite; a program needn't handle non-finite values.
Results may differ from a plain program's by a relative error of at most 0.0001.
Values sent between devices are 32-bit elements; how exact they have to be, the bound alone decides.
A program may use at most 128 MiB of HBM per device.

v0:
```python
import math

import jax
import jax.numpy as jnp
from jax import lax
from jax.sharding import PartitionSpec as P

NF = 64
NK = 64
MODES = 4096


KAPPA = 0.2
COUPLING = 0.5
HIGHEST = lax.Precision.HIGHEST


def with_halo(block, sides, width):
    for axis, dim in sides:
        count = lax.axis_size(axis)
        forward = [(i, i + 1) for i in range(count - 1)]
        backward = [(target, source) for source, target in forward]
        low = lax.ppermute(
            lax.slice_in_dim(block, block.shape[dim] - width, None, axis=dim), axis, forward
        )
        high = lax.ppermute(lax.slice_in_dim(block, 0, width, axis=dim), axis, backward)
        block = jnp.concatenate([low, block, high], axis=dim)
    return block


def entering(value, axis, join, neutral):
    count, mine = (lax.axis_size(axis), lax.axis_index(axis))
    pieces = lax.all_gather(value, axis)
    so_far = jnp.full_like(value, 0) + jnp.asarray(neutral, value.dtype)

    def turn(position, so_far):
        longer = join(so_far, pieces[position])
        return jnp.where(position < mine, longer, so_far)

    return lax.fori_loop(0, count - 1, turn, so_far)


def add_pair(earlier, later):
    return earlier + later


def rates(grid_index):
    freq_index = grid_index // NK
    span_index = grid_index % NK
    freq_signed = (freq_index + NF // 2) % NF - NF // 2
    span_signed = (span_index + NK // 2) % NK - NK // 2
    return (2.0 / NF * freq_signed.astype(jnp.float32), 2.0 / NK * span_signed.astype(jnp.float32))


def span_tables(direction):
    col_ids = jnp.arange(NK, dtype=jnp.int32)
    phase_cols = 2.0 * math.pi / NK * (col_ids[:, None] * col_ids[None, :] % NK).astype(jnp.float32)
    return (jnp.cos(phase_cols), direction * jnp.sin(phase_cols))


def row_tables(direction, out_ids, in_ids):
    phase_rows = 2.0 * math.pi / NF * (out_ids[:, None] * in_ids[None, :] % NF).astype(jnp.float32)
    return (jnp.cos(phase_rows), direction * jnp.sin(phase_rows))


def span_dft(real_part, imag_part, direction):
    cosine, sine_part = span_tables(direction)
    real_cos = jnp.einsum("...k,kz->...z", real_part, cosine, precision=HIGHEST)
    real_sin = jnp.einsum("...k,kz->...z", real_part, sine_part, precision=HIGHEST)
    imag_cos = jnp.einsum("...k,kz->...z", imag_part, cosine, precision=HIGHEST)
    imag_sin = jnp.einsum("...k,kz->...z", imag_part, sine_part, precision=HIGHEST)
    return (real_cos - imag_sin, real_sin + imag_cos)


def lead_dft(real_part, imag_part, direction, out_ids, in_ids):
    cos_rows, sin_rows = row_tables(direction, out_ids, in_ids)
    lead_shape = real_part.shape
    flat_real = real_part.reshape(lead_shape[0], -1)
    flat_imag = imag_part.reshape(lead_shape[0], -1)
    out_real = jnp.dot(cos_rows, flat_real, precision=HIGHEST) - jnp.dot(
        sin_rows, flat_imag, precision=HIGHEST
    )
    out_imag = jnp.dot(sin_rows, flat_real, precision=HIGHEST) + jnp.dot(
        cos_rows, flat_imag, precision=HIGHEST
    )
    return (out_real.reshape(lead_shape), out_imag.reshape(lead_shape))


def to_physical(real_part, imag_part, out_ids, in_ids):
    shape_front = real_part.shape[:-1] + (NF, NK)
    span_real, span_imag = span_dft(
        real_part.reshape(shape_front), imag_part.reshape(shape_front), 1.0
    )
    span_real = jnp.moveaxis(span_real, -2, 0)
    span_imag = jnp.moveaxis(span_imag, -2, 0)
    return lead_dft(span_real, span_imag, 1.0, out_ids, in_ids)


def to_spectral(real_part, imag_part, out_ids, in_ids):
    lead_real, lead_imag = lead_dft(real_part, imag_part, -1.0, out_ids, in_ids)
    lead_real = jnp.moveaxis(lead_real, 0, -2)
    lead_imag = jnp.moveaxis(lead_imag, 0, -2)
    span_real, span_imag = span_dft(lead_real, lead_imag, -1.0)
    shape_front = span_real.shape[:-2] + (MODES,)
    return (span_real.reshape(shape_front), span_imag.reshape(shape_front))


def coupling_term(adjoint_slots, forward_phys, block_freq, time_ids):
    a_real, a_imag = to_physical(adjoint_slots[0], adjoint_slots[1], time_ids, block_freq)
    w_real = forward_phys[0][:, None]
    w_imag = forward_phys[1][:, None]
    prod_real = w_real * a_real + w_imag * a_imag
    prod_imag = w_real * a_imag - w_imag * a_real
    real_part, imag_part = to_spectral(prod_real, prod_imag, block_freq, time_ids)
    return jnp.stack([real_part, imag_part]) / (NF * NK)


def add_continuity(stepped, running, row_scale):
    updated_v = jnp.stack(
        [stepped[0, 1] + running[1] * row_scale, stepped[1, 1] - running[0] * row_scale]
    )
    return jnp.concatenate([stepped[:, :1], updated_v[:, None], stepped[:, 2:]], 1)


def wall_step_modes(current, coupled, alpha_rate, beta_rate, row_scale):
    padded = with_halo(current, ((("wall", "ckpt"), 2),), 1)
    stepped = (
        current
        + KAPPA * (padded[:, :, 2:] - 2.0 * current + padded[:, :, :-2])
        - COUPLING * coupled
    )
    source = alpha_rate * stepped[:, 0] + beta_rate * stepped[:, 2]
    row_count = current.shape[2]
    row_ids = jnp.arange(row_count, dtype=jnp.int32)
    lower_ones = (row_ids[:, None] >= row_ids[None, :]).astype(jnp.float32)
    running = jnp.einsum("yv,cvm->cym", lower_ones, source, precision=HIGHEST)
    totals = running[:, -1]
    before = entering(totals, ("wall", "ckpt"), add_pair, jnp.zeros_like(totals))
    running = running + before[:, None]
    return add_continuity(stepped, running, row_scale)


def to_modes(values):
    return lax.all_to_all(values, "mode", split_axis=3, concat_axis=2, tiled=True)


def on_device(adjoint, forward, mode_map):
    station_count = lax.axis_size("ckpt")
    row_scale = 1.0 / math.sqrt(adjoint.shape[2] * lax.axis_size("wall") * lax.axis_size("ckpt"))
    stored = lax.all_gather(forward, "ckpt", axis=0, tiled=True)
    row_count = adjoint.shape[2]
    own_rows = lax.dynamic_slice_in_dim(stored, lax.axis_index("ckpt") * row_count, row_count, 2)
    full_map = lax.all_gather(mode_map, "mode", axis=0, tiled=True)
    block_freq = full_map.reshape(NF, NK)[:, 0] // NK
    time_ids = jnp.arange(NF, dtype=jnp.int32)
    adjoint_cols, forward_cols = (
        lax.all_to_all(adjoint, "mode", split_axis=2, concat_axis=3, tiled=True),
        lax.all_to_all(own_rows, "mode", split_axis=2, concat_axis=3, tiled=True),
    )
    phys_real, phys_imag = to_physical(forward_cols[:, 0], forward_cols[:, 1], time_ids, block_freq)
    local_alpha, local_beta = rates(mode_map)
    current = adjoint
    for station in range(station_count - 1, -1, -1):
        if station == station_count - 1:
            columns = adjoint_cols
        else:
            columns = lax.all_to_all(current, "mode", split_axis=2, concat_axis=3, tiled=True)
        station_phys = (phys_real[:, station], phys_imag[:, station])
        coupled = to_modes(coupling_term(columns, station_phys, block_freq, time_ids))
        current = wall_step_modes(current, coupled, local_alpha, local_beta, row_scale)
    return current


def solution(mesh):
    placed = (P(None, None, ("wall", "ckpt"), "mode"), P("ckpt", None, "wall", "mode"), P("mode"))
    return jax.shard_map(
        on_device,
        mesh=mesh,
        in_specs=placed,
        out_specs=P(None, None, ("wall", "ckpt"), "mode"),
        check_vma=False,
    )
```

profile of v0, /device:TPU:1, one launch (start us, length us, event | category | flops | bytes accessed | tf_op | source)
XLA Modules:
  0.0 544.7 jit_solution(10773207464401871965)
XLA Ops:
  6.5 3.5 copy.215
  10.0 8.7 %all-to-all-start.1 = ((f32[2,5,256,128]{3,1,0,2:T(8,128)}), f32[2,5,256,128]{3,1,0,2:T(8,128)S(1)}, u32[]{:S(2)}, u32[]{:S(2)}) async-start(f32[2,5,256,128]{3,1,0,2:T(8,128)} %copy.215), calls=%async_computation.1 | async-start | bytes 4194304 | tf_op jit(solution)/shard_map/all_to_all | solution.py:157
  19.5 40.0 %all-gather.2 = s32[32,1,128]{2,1,0:T(1,128)S(1)} all-gather(s32[1,1,128]{2,1,0:T(1,128)S(1)} %bitcast.305), channel_id=1, replica_groups=mesh['mode'=32,'wall'=2,'ckpt'=2] {'mode'}, dimensions={0}, use_global_device_ids=true | all-gather | bytes 16896 | tf_op jit(solution)/shard_map/all_gather | solution.py:153
  63.2 5.6 %all-to-all-start = ((f32[2,2,256,128]{3,1,0,2:T(2,128)}), f32[2,2,256,128]{3,1,0,2:T(2,128)}, u32[]{:S(2)}, u32[]{:S(2)}) async-start(f32[2,2,256,128]{3,1,0,2:T(2,128)} %copy.211), calls=%async_computation | async-start | bytes 1048576 | tf_op jit(solution)/shard_map/all_to_all | solution.py:158
  70.0 5.1 fusion.64
  75.1 5.1 fusion.76
  81.5 4.0 convolution_subtract_fusion.7
  85.6 4.0 convolution_add_fusion.7
  89.6 2.2 fusion.144
  93.4 2.5 convolution_add_fusion.3
  99.7 1.7 fusion.24
  114.2 3.2 multiply_subtract_fusion.1
  117.4 1.9 fusion.99
  121.5 2.4 fusion.21
  125.2 1.7 convolution_add_fusion.2
  128.3 3.7 convolution_subtract_fusion.6
  132.1 1.7 stack_reshape.12
  133.8 2.4 convolution_add_fusion.6
  136.2 1.7 stack_reshape.13
  138.1 17.9 %copy.223 = f32[2,5,8,4096]{2,0,1,3:T(2,128)} copy(f32[2,5,8,4096]{3,2,1,0:T(8,128)S(1)} %maximum_multiply_fusion) | data formatting | bytes 2621440 | tf_op jit(solution)/shard_map/div | solution.py:115
  155.9 31.2 %reshape.142 = f32[32,1,10240]{2,1,0:T(1,128)} reshape(f32[4096,5,2,8]{3,2,1,0:T(2,128)} %bitcast.284) | data formatting | bytes 2621440
  187.1 7.6 %all-to-all-start.2 = ((f32[32,1,10240]{2,1,0:T(1,128)}), f32[32,1,10240]{2,1,0:T(1,128)}, u32[]{:S(2)}, u32[]{:S(2)}) async-start(f32[32,1,10240]{2,1,0:T(1,128)} %reshape.142), calls=%async_computation.2 | async-start | bytes 2621440 | tf_op jit(solution)/shard_map/all_to_all | solution.py:144
  196.0 6.1 %collective-permute-start.1 = (f32[2,5,1,128]{3,0,2,1:T(2,128)S(1)}, f32[2,5,1,128]{3,0,2,1:T(2,128)S(1)}, u32[]{:S(2)}, u32[]{:S(2)}) collective-permute-start(f32[2,5,1,128]{3,0,2,1:T(2,128)S(1)} %copy.261), channel_id=1, source_target_pairs={{0,1},{1,2},{2,3},{4,5},{5,6},{6,7},{8,9},{9,10},{10,11},{12,13},{... | collective-permute-start | bytes 15368 | tf_op jit(solution)/shard_map/ppermute | solution.py:23
  204.0 10.5 %all-to-all-done.2 = f32[32,1,10240]{2,1,0:T(1,128)} async-done(((f32[32,1,10240]{2,1,0:T(1,128)}), f32[32,1,10240]{2,1,0:T(1,128)}, u32[]{:S(2)}, u32[]{:S(2)}) %all-to-all-start.2) | async-done | bytes 1310752 | tf_op jit(solution)/shard_map/all_to_all | solution.py:144
  215.1 5.1 reduce.4
  220.1 41.4 %reshape.143 = f32[4096,5,2,8]{3,2,1,0:T(2,128)} reshape(f32[32,10240]{1,0:T(8,128)S(1)} %reduce.4) | data formatting | bytes 2621440
  261.5 21.6 %copy.224 = f32[2,5,8,4096]{3,2,1,0:T(8,128)S(1)} copy(f32[2,5,8,4096]{2,0,1,3:T(2,128)} %bitcast.285) | data formatting | bytes 2621440 | tf_op jit(solution)/shard_map/all_to_all | solution.py:144
  285.7 2.4 fusion.9
  288.8 9.3 %all-gather = f32[8,1,128]{2,1,0:T(1,128)S(1)} all-gather(f32[2,1,128]{2,1,0:T(1,128)S(1)} %copy.227), channel_id=2, replica_groups=mesh['mode'=32,'wall'=2,'ckpt'=2] {'wall','ckpt'}, dimensions={0}, use_global_device_ids=true | all-gather | bytes 5120 | tf_op jit(solution)/shard_map/all_gather | solution.py:33
  299.0 2.1 copy.232
  301.2 6.0 %all-to-all-start.3 = ((f32[2,5,256,128]{3,0,1,2:T(2,128)}), f32[2,5,256,128]{3,0,1,2:T(2,128)S(1)}, u32[]{:S(2)}, u32[]{:S(2)}) async-start(f32[2,5,256,128]{3,0,1,2:T(2,128)} %copy.232), calls=%async_computation.3 | async-start | bytes 2621440 | tf_op jit(solution)/shard_map/all_to_all | solution.py:167
  307.2 2.1 mul.489
  309.3 2.5 mul.490
  311.8 2.1 mul.493
  313.9 2.5 mul.494
  316.4 10.6 %all-to-all-done.3 = f32[2,5,256,128]{3,0,1,2:T(2,128)S(1)} async-done(((f32[2,5,256,128]{3,0,1,2:T(2,128)}), f32[2,5,256,128]{3,0,1,2:T(2,128)S(1)}, u32[]{:S(2)}, u32[]{:S(2)}) %all-to-all-start.3) | async-done | bytes 1310752 | tf_op jit(solution)/shard_map/all_to_all | solution.py:167
  330.2 2.4 fusion.79
  332.6 2.4 fusion.69
  337.3 2.6 fusion
  339.9 1.8 copy.236
  341.7 2.5 reshape.116
  344.2 2.9 fusion.141
  350.0 1.8 copy.237
  351.8 1.7 reshape.117
  355.9 2.0 multiply_subtract_fusion
  358.0 1.8 fusion.98
  360.6 1.8 convolution_subtract_fusion
  363.7 2.4 fusion.15
  366.2 2.4 fusion.13
  368.6 1.7 convolution_add_fusion
  371.7 3.7 convolution_subtract_fusion.4
  375.4 2.6 stack_reshape.14
  378.0 3.7 convolution_add_fusion.4
  381.7 2.6 stack_reshape.15
  385.7 17.9 %copy.240 = f32[2,5,8,4096]{2,0,1,3:T(2,128)} copy(f32[2,5,8,4096]{3,2,1,0:T(8,128)S(1)} %maximum_multiply_fusion.1) | data formatting | bytes 2621440 | tf_op jit(solution)/shard_map/div | solution.py:115
  403.5 31.4 %reshape.144 = f32[32,1,10240]{2,1,0:T(1,128)} reshape(f32[4096,5,2,8]{3,2,1,0:T(2,128)} %bitcast.286) | data formatting | bytes 2621440
  434.9 3.8 all-to-all-start.4
  444.0 5.5 %collective-permute-start.3 = (f32[2,5,1,128]{3,0,2,1:T(2,128)S(1)}, f32[2,5,1,128]{3,0,2,1:T(2,128)S(1)}, u32[]{:S(2)}, u32[]{:S(2)}) collective-permute-start(f32[2,5,1,128]{3,0,2,1:T(2,128)S(1)} %copy.230), channel_id=1, source_target_pairs={{0,1},{1,2},{2,3},{4,5},{5,6},{6,7},{8,9},{9,10},{10,11},{12,13},{... | collective-permute-start | bytes 15368 | tf_op jit(solution)/shard_map/ppermute | solution.py:23
  451.8 6.9 %all-to-all-done.4 = f32[32,1,10240]{2,1,0:T(1,128)S(1)} async-done(((f32[32,1,10240]{2,1,0:T(1,128)}), f32[32,1,10240]{2,1,0:T(1,128)S(1)}, u32[]{:S(2)}, u32[]{:S(2)}) %all-to-all-start.4) | async-done | bytes 1310752 | tf_op jit(solution)/shard_map/all_to_all | solution.py:144
  458.6 3.7 reduce.5
  462.4 41.1 %reshape.145 = f32[4096,5,2,8]{3,2,1,0:T(2,128)} reshape(f32[32,10240]{1,0:T(8,128)S(1)} %reduce.5) | data formatting | bytes 2621440
  503.5 21.6 %copy.241 = f32[2,5,8,4096]{3,2,1,0:T(8,128)S(1)} copy(f32[2,5,8,4096]{2,0,1,3:T(2,128)} %bitcast.287) | data formatting | bytes 2621440 | tf_op jit(solution)/shard_map/all_to_all | solution.py:144
  526.7 2.7 copy_subtract_fusion
  530.0 5.8 %all-gather.1 = f32[8,1,128]{2,1,0:T(1,128)S(1)} all-gather(f32[2,1,128]{2,1,0:T(1,128)S(1)} %copy.246), channel_id=3, replica_groups=mesh['mode'=32,'wall'=2,'ckpt'=2] {'wall','ckpt'}, dimensions={0}, use_global_device_ids=true | all-gather | bytes 5120 | tf_op jit(solution)/shard_map/all_gather | solution.py:33
  (154 shorter events, 65.1 us)
Async XLA Ops:
  10.0 9.5 %copy-start.18 = (s32[128]{0:T(128)S(1)}, s32[128]{0:T(128)}, u32[]{:S(2)}) copy-start(s32[128]{0:T(128)} %param.9) | copy-start | bytes 1540
  10.0 53.2 %all-to-all-start.1 = ((f32[2,5,256,128]{3,1,0,2:T(8,128)}), f32[2,5,256,128]{3,1,0,2:T(8,128)S(1)}, u32[]{:S(2)}, u32[]{:S(2)}) async-start(f32[2,5,256,128]{3,1,0,2:T(8,128)} %copy.215), calls=%async_computation.1 | async-start | bytes 4194304 | tf_op jit(solution)/shard_map/all_to_all | solution.py:157
  18.7 42.2 %all-gather.5.cloned.1.call-start = ((), (), s32[]{:S(2)}) async-start(), calls=%async_computation.5 | async-start | bytes 1572864 | tf_op jit(solution)/shard_map/all_gather | solution.py:150
  63.2 32.7 %all-to-all-start = ((f32[2,2,256,128]{3,1,0,2:T(2,128)}), f32[2,2,256,128]{3,1,0,2:T(2,128)}, u32[]{:S(2)}, u32[]{:S(2)}) async-start(f32[2,2,256,128]{3,1,0,2:T(2,128)} %copy.211), calls=%async_computation | async-start | bytes 1048576 | tf_op jit(solution)/shard_map/all_to_all | solution.py:158
  80.2 1.3 copy-start.7
  81.5 4.0 copy-start.6
  106.9 1.0 copy-start.17
  123.9 1.3 copy-start.13
  187.1 7.6 %copy-start.4 = (f32[2,5,256,128]{3,2,1,0:T(8,128)S(1)}, f32[2,5,256,128]{3,2,1,0:T(8,128)}, u32[]{:S(2)}) copy-start(f32[2,5,256,128]{3,2,1,0:T(8,128)} %param.7) | copy-start | bytes 3932164
  187.1 27.4 %all-to-all-start.2 = ((f32[32,1,10240]{2,1,0:T(1,128)}), f32[32,1,10240]{2,1,0:T(1,128)}, u32[]{:S(2)}, u32[]{:S(2)}) async-start(f32[32,1,10240]{2,1,0:T(1,128)} %reshape.142), calls=%async_computation.2 | async-start | bytes 2621440 | tf_op jit(solution)/shard_map/all_to_all | solution.py:144
  194.7 7.9 %collective-permute-start = (f32[2,5,1,128]{3,0,2,1:T(2,128)S(1)}, f32[2,5,1,128]{3,0,2,1:T(2,128)S(1)}, u32[]{:S(2)}, u32[]{:S(2)}) collective-permute-start(f32[2,5,1,128]{3,0,2,1:T(2,128)S(1)} %copy.260), channel_id=1, source_target_pairs={{1,0},{2,1},{3,2},{5,4},{6,5},{7,6},{9,8},{10,9},{11,10},{13,12},{... | collective-permute-start | bytes 15368 | tf_op jit(solution)/shard_map/ppermute | solution.py:26
  196.0 6.9 %collective-permute-start.1 = (f32[2,5,1,128]{3,0,2,1:T(2,128)S(1)}, f32[2,5,1,128]{3,0,2,1:T(2,128)S(1)}, u32[]{:S(2)}, u32[]{:S(2)}) collective-permute-start(f32[2,5,1,128]{3,0,2,1:T(2,128)S(1)} %copy.261), channel_id=1, source_target_pairs={{0,1},{1,2},{2,3},{4,5},{5,6},{6,7},{8,9},{9,10},{10,11},{12,13},{... | collective-permute-start | bytes 15368 | tf_op jit(solution)/shard_map/ppermute | solution.py:23
  288.2 10.1 %copy-start.15 = (f32[2,1,256,128]{2,3,0,1:T(8,128)}, f32[2,1,256,128]{2,3,0,1:T(8,128)S(1)}, u32[]{:S(2)}) copy-start(f32[2,1,256,128]{2,3,0,1:T(8,128)S(1)} %slice.157) | copy-start | bytes 786436
  298.3 0.7 copy-start.16
  301.2 25.7 %all-to-all-start.3 = ((f32[2,5,256,128]{3,0,1,2:T(2,128)}), f32[2,5,256,128]{3,0,1,2:T(2,128)S(1)}, u32[]{:S(2)}, u32[]{:S(2)}) async-start(f32[2,5,256,128]{3,0,1,2:T(2,128)} %copy.232), calls=%async_computation.3 | async-start | bytes 2621440 | tf_op jit(solution)/shard_map/all_to_all | solution.py:167
  332.6 2.4 copy-start.9
  344.2 2.9 copy-start.3
  344.2 4.5 copy-start.5
  351.8 2.6 copy-start.14
  353.6 0.8 copy-start.2
  354.4 1.1 copy-start.8
  354.4 1.3 copy-start.10
  354.4 1.5 copy-start.11
  357.9 2.7 copy-start
  366.2 2.4 copy-start.1
  366.2 2.4 copy-start.12
  434.9 23.7 %all-to-all-start.4 = ((f32[32,1,10240]{2,1,0:T(1,128)}), f32[32,1,10240]{2,1,0:T(1,128)S(1)}, u32[]{:S(2)}, u32[]{:S(2)}) async-start(f32[32,1,10240]{2,1,0:T(1,128)} %reshape.144), calls=%async_computation.4 | async-start | bytes 2621440 | tf_op jit(solution)/shard_map/all_to_all | solution.py:144
  441.4 8.1 %collective-permute-start.2 = (f32[2,5,1,128]{3,0,2,1:T(2,128)S(1)}, f32[2,5,1,128]{3,0,2,1:T(2,128)S(1)}, u32[]{:S(2)}, u32[]{:S(2)}) collective-permute-start(f32[2,5,1,128]{3,0,2,1:T(2,128)S(1)} %copy.228), channel_id=1, source_target_pairs={{1,0},{2,1},{3,2},{5,4},{6,5},{7,6},{9,8},{10,9},{11,10},{13,12},{... | collective-permute-start | bytes 15368 | tf_op jit(solution)/shard_map/ppermute | solution.py:26
  444.0 6.7 %collective-permute-start.3 = (f32[2,5,1,128]{3,0,2,1:T(2,128)S(1)}, f32[2,5,1,128]{3,0,2,1:T(2,128)S(1)}, u32[]{:S(2)}, u32[]{:S(2)}) collective-permute-start(f32[2,5,1,128]{3,0,2,1:T(2,128)S(1)} %copy.230), channel_id=1, source_target_pairs={{0,1},{1,2},{2,3},{4,5},{5,6},{6,7},{8,9},{9,10},{10,11},{12,13},{... | collective-permute-start | bytes 15368 | tf_op jit(solution)/shard_map/ppermute | solution.py:23
Sparse Core Ops, SparseCore 0:
  21.2 27.2 all-gather.4
where the time goes:
time: 551 us; the launch traced here: 545 us
  local copies, waits for them, and re-layouts  296 us (54%)
  matrix products  87.6 us (16%)
  blocking collectives  55.1 us (10%)
  starting transfers between devices  46 us (8%)
  waiting for transfers between devices  28.7 us (5%)
  other arithmetic  16.9 us (3%)
  between operations  14.4 us (3%)
    unnamed x49, local copies, waits for them, and re-layouts  153 us
    all_to_all x3, local copies, waits for them, and re-layouts, to_modes(): lax.all_to_all(values, 'mode', split_axis=3, concat_axis=2, tiled=True)  43.7 us
    all_gather x1, blocking collectives, on_device(): full_map = lax.all_gather(mode_map, 'mode', axis=0, tiled=True)  40 us
    div x2, local copies, waits for them, and re-layouts, coupling_term(): return jnp.stack([real_part, imag_part]) / (NF * NK)  35.7 us
    all_to_all x2, waiting for transfers between devices, to_modes(): lax.all_to_all(values, 'mode', split_axis=3, concat_axis=2, tiled=True)  17.4 us
    dot_general x5, matrix products, span_dft(): jnp.einsum('...k,kz->...z', imag_part, sine_part, precision=HIGHEST)  15.8 us
    all_gather x2, blocking collectives, entering(): pieces = lax.all_gather(value, axis)  15.1 us
    dot_general x5, matrix products, span_dft(): real_cos = jnp.einsum('...k,kz->...z', real_part, cosine, precision=HIGHEST)  13.8 us
  transfers between devices with their start and end apart: 10, of which 3 were waited for; matrix products, arithmetic and copies ran while one was open for 9% of the time, Pallas kernels for 0%

commit v1 on v0

v1 whole, which is shorter than its diff:
```python
import functools

import jax
import jax.numpy as jnp
import numpy as np
from jax import lax
from jax.experimental import pallas as pl
from jax.experimental.pallas import tpu as pltpu
from jax.sharding import PartitionSpec as P

NF = 64
NK = 64
NY = 1024
PEERS = 32
ROWS = 256
F32 = jnp.float32
BF16 = jnp.bfloat16
MESH = pl.DeviceIdType.MESH

IN = {2: 0, 0: 1, 3: 3, 4: 5, 1: 6}
F_OWN, F_OTHER, MID, BACK = 2, 4, 7, 8
OUT = {0: 9, 2: 10, 3: 11, 4: 12, 1: 13}
SLOTS = 14


def hi_lo(table):
    hi = table.astype(np.float32).astype(BF16)
    lo = (table - hi.astype(np.float64)).astype(np.float32).astype(BF16)
    return jnp.asarray(hi), jnp.asarray(lo)


def complex_blocks(cosine, sine):
    return np.stack([np.stack([cosine, -sine]), np.stack([sine, cosine])])


def tables():
    ids = np.arange(64)
    angle = 2.0 * np.pi / 64 * (ids[:, None] * ids[None, :] % 64)
    cosine, sine = np.cos(angle), np.sin(angle)
    blocks = complex_blocks(cosine, sine)
    eye = np.eye(2)
    span = np.einsum("pqzk,ab->zpaqbk", blocks, eye).reshape(256, 256)
    time = np.einsum("pqtg,ab->patbqg", blocks, eye).reshape(256, 256)
    signed = (ids + 32) % 64 - 32
    beta = 2.0 * signed / 64
    lag = ids[:, None] - ids[None, :]
    wave = np.exp(2j * np.pi / 64 * (lag[:, :, None] * ids % 64))
    slope = (-1j / np.sqrt(NY)) * (wave * beta).sum(-1) / 64
    deriv = np.einsum(
        "pqzx,ab->zpaxqb", complex_blocks(slope.real, slope.imag), eye
    ).reshape(256, 256)
    upto = (np.arange(256)[:, None] <= np.arange(256)[None, :]).astype(np.float32)
    return (
        *hi_lo(span),
        *hi_lo(time),
        *hi_lo(-time.T / 128),
        *hi_lo(deriv),
        jnp.asarray(upto.astype(BF16)),
        jnp.asarray(upto.T.astype(BF16)),
    )


def split(x):
    hi = x.astype(BF16)
    return hi, (x - hi.astype(F32)).astype(BF16)


def dot(a, b, ca=1, cb=0):
    return lax.dot_general(a, b, (((ca,), (cb,)), ((), ())), preferred_element_type=F32)


def kernel(
    map_s, map_v, adj, fwd, span_h, span_l, time_h, time_l, inv_h, inv_l, der_h, der_l,
    upper, lower, out,
    xin, fin, fz, ptile, ptab, sb, db, es, eh, tb, ft, ftb, tm, ti, amp, phys, qs, stage,
    load_sem, fload_sem, fz_sem, p_sem, ssem, rsem, es_sem, er_sem, tt_sem, ft_sem, st_sem,
):
    me = lax.axis_index("mode")
    wall, ckpt = lax.axis_index("wall"), lax.axis_index("ckpt")
    mx, my, mc = me // 8, (me // 2) % 4, me % 2
    rank = wall * 2 + ckpt

    def peer(i):
        return ((mx + i // 8) % 4) * 8 + ((my + (i // 2) % 4) % 4) * 2 + (mc + i % 2) % 2

    def plane(offset):
        other = (rank + offset) % 4
        return {"wall": other // 2, "ckpt": other % 2}

    bar = pltpu.get_barrier_semaphore()

    def greet(i, carry):
        pl.semaphore_signal(bar, inc=1, device_id={"mode": peer(i)}, device_id_type=MESH)
        return carry

    lax.fori_loop(1, PEERS, greet, 0)
    for o in (1, 2, 3):
        pl.semaphore_signal(bar, inc=1, device_id=plane(o), device_id_type=MESH)

    loads = {}
    for c in (2, 0, 3, 4, 1):
        loads[c] = pltpu.make_async_copy(adj.at[:, c], xin.at[c], load_sem.at[c])
        loads[c].start()
    load_f = pltpu.make_async_copy(
        fwd.at[0, :, pl.ds(ckpt * ROWS, ROWS)], fin, fload_sem
    )
    load_f.start()

    row8 = lax.broadcasted_iota(jnp.int32, (8, 128), 0)
    ptile[...] = jnp.where(row8 % 2 == 0, map_s[0, 0] >> 6, map_s[0, 64] >> 6)

    pl.semaphore_wait(bar, PEERS - 1 + 3)

    send_fz = pltpu.make_async_remote_copy(
        fwd.at[0, :, pl.ds((1 - ckpt) * ROWS, ROWS)], fz, fz_sem.at[0], fz_sem.at[1],
        device_id={"ckpt": 1 - ckpt}, device_id_type=MESH,
    )
    send_fz.start()

    def send_p(i, carry):
        p = peer(i)
        pltpu.make_async_remote_copy(
            ptile, ptab.at[me], p_sem.at[0], p_sem.at[1],
            device_id={"mode": p}, device_id_type=MESH,
        ).start()
        return carry

    lax.fori_loop(1, PEERS, send_p, 0)
    ptab[me] = ptile[...]

    def exchange(k, value):
        sb[k] = value.reshape(PEERS, 8, ROWS)

        def one(i, carry):
            p = peer(i)
            pltpu.make_async_remote_copy(
                sb.at[k, p], db.at[k, me], ssem.at[k], rsem.at[k],
                device_id={"mode": p}, device_id_type=MESH,
            ).start()
            return carry

        lax.fori_loop(1, PEERS, one, 0)
        db[k, me] = sb[k, me]

    def whole(k):
        n = pl.ds(0, PEERS - 1)
        return pltpu.make_async_remote_copy(
            sb.at[k, n], db.at[k, n], ssem.at[k], rsem.at[k],
            device_id={"mode": peer(1)}, device_id_type=MESH,
        )

    def arrived(k):
        whole(k).wait_recv()
        return db[k].reshape(ROWS, ROWS)

    def dot3(ah, al, x, cb=0):
        xh, xl = split(x)
        return dot(ah[...], xh, 1, cb) + dot(ah[...], xl, 1, cb) + dot(al[...], xh, 1, cb)

    def to_span(real, imag):
        return dot3(span_h, span_l, jnp.concatenate([real, imag], 1), 1)

    def send_field(c):
        loads[c].wait()
        exchange(IN[c], to_span(xin[c, 0], xin[c, 1]))

    send_field(2)
    send_field(0)
    load_f.wait()
    exchange(F_OWN, to_span(fin[0], fin[1]))
    send_field(3)

    n = pl.ds(0, PEERS - 1)
    wait_p = pltpu.make_async_remote_copy(
        ptab.at[n], ptab.at[n], p_sem.at[0], p_sem.at[1],
        device_id={"mode": peer(1)}, device_id_type=MESH,
    )
    wait_p.wait_recv()
    freq = ptab[...].reshape(ROWS, 128)
    row = lax.broadcasted_iota(jnp.int32, (ROWS, 128), 0)
    lane = lax.broadcasted_iota(jnp.int32, (ROWS, 128), 1)
    inside = (row % 8) // 2
    onehot = jnp.concatenate(
        [
            jnp.where(inside * 64 + freq == lane + half * 128, 1.0, 0.0)
            for half in (0, 1)
        ],
        1,
    ).astype(BF16)
    tm[0] = dot(time_h[...], onehot, 1, 1).astype(BF16)
    tm[1] = dot(time_l[...], onehot, 1, 1).astype(BF16)
    ti[0] = dot(onehot, inv_h[...]).astype(BF16)
    ti[1] = dot(onehot, inv_l[...]).astype(BF16)
    signed = jnp.where(freq >= 32, freq - 64, freq).astype(F32) * (1.0 / 1024)
    amp[...] = jnp.where((row // 2) % 2 == 0, signed, -signed)

    first, last = lane == 0, lane == 127
    has_low = (rank > 0).astype(F32)
    has_high = (rank < 3).astype(F32)

    def edge_copies(j):
        return [
            pltpu.make_async_remote_copy(
                es.at[j, s], eh.at[j, s], es_sem.at[j, s], er_sem.at[j, s],
                device_id=plane(o), device_id_type=MESH,
            )
            for s, o in ((0, 1), (1, 3))
        ]

    def send_edges(j, x):
        comb = jnp.where(
            last,
            pltpu.roll(x[:, :128], 127, 1),
            jnp.where(first, pltpu.roll(x[:, 128:], 1, 1), 0.0),
        ).T
        es[j, 0] = comb[:8]
        es[j, 1] = comb[120:]
        for copy in edge_copies(j):
            copy.start()

    def smoothed(x, low, high):
        halo = jnp.concatenate([low, jnp.zeros((112, ROWS), F32), high]).T
        xl, xh = x[:, :128], x[:, 128:]
        dl, dh = pltpu.roll(xl, 1, 1), pltpu.roll(xh, 1, 1)
        ul, uh = pltpu.roll(xl, 127, 1), pltpu.roll(xh, 127, 1)
        below = jnp.concatenate([jnp.where(first, halo, dl), jnp.where(first, dl, dh)], 1)
        above = jnp.concatenate([jnp.where(last, uh, ul), jnp.where(last, halo, uh)], 1)
        return x + 0.2 * ((above - 2.0 * x) + below)

    def to_time(x):
        return dot3(tm.at[0], tm.at[1], x)

    def prepare(c, x, j):
        send_edges(j, x)
        amp_phys = to_time(x)
        phys[c] = amp_phys

    def coupled(c, s):
        ar, ai = phys[c, :128], phys[c, 128:]
        fr, fi = phys[5 + s, :128], phys[5 + s, 128:]
        prod = jnp.concatenate([fr * ar + fi * ai, fr * ai - fi * ar])
        return dot3(ti.at[0], ti.at[1], prod)

    def step(c, x, s, j):
        term = coupled(c, s)
        for copy in edge_copies(j):
            copy.wait_recv()
        return smoothed(x, eh[j, 0] * has_low, eh[j, 1] * has_high) + term

    def first_step(c):
        qs[c] = step(c, db[IN[c]].reshape(ROWS, ROWS), 1, c)

    def begin(c):
        prepare(c, arrived(IN[c]), c)

    def again(c):
        prepare(c, qs[c], 5 + c)

    def finish(c):
        exchange(OUT[c], step(c, qs[c], 0, 5 + c))

    begin(2)
    begin(0)
    send_fz.wait_recv()
    exchange(F_OTHER, to_span(fz[0], fz[1]))
    send_field(4)
    send_field(1)
    phys[5 + ckpt] = to_time(arrived(F_OWN))
    begin(3)
    phys[6 - ckpt] = to_time(arrived(F_OTHER))
    first_step(2)
    exchange(MID, qs[2])
    first_step(0)
    again(0)
    again(2)
    begin(4)
    finish(0)
    first_step(3)
    again(3)
    finish(2)
    exchange(BACK, dot3(der_h, der_l, arrived(MID)))
    first_step(4)
    again(4)
    begin(1)
    first_step(1)
    finish(3)
    finish(4)

    u1 = qs[0]
    row2 = lax.broadcasted_iota(jnp.int32, (ROWS, ROWS), 0)
    turned = jnp.where(
        (row2 // 2) % 2 == 0, pltpu.roll(u1, ROWS - 2, 0), pltpu.roll(u1, 2, 0)
    )
    source = turned * jnp.concatenate([amp[...], amp[...]], 1) + arrived(BACK)
    sh, sl = split(source)
    running = dot(sh, upper[...]) + dot(sl, upper[...])
    v1 = qs[1] + running
    j = 6
    second = lane == 1
    comb = jnp.where(
        last,
        pltpu.roll(v1[:, :128], 127, 1),
        jnp.where(
            first,
            pltpu.roll(v1[:, 128:], 1, 1),
            jnp.where(second, pltpu.roll(running[:, 128:], 2, 1), 0.0),
        ),
    ).T
    es[j, 0] = comb[:8]
    es[j, 1] = comb[120:]
    for copy in edge_copies(j):
        copy.start()
    totals = [
        pltpu.make_async_remote_copy(
            es.at[j, 0], tb.at[o - 2], tt_sem.at[0, o - 2], tt_sem.at[1, o - 2],
            device_id=plane(o), device_id_type=MESH,
        )
        for o in (2, 3)
    ]
    for copy in totals:
        copy.start()
    mine = comb[:8]
    for copy in edge_copies(j) + totals:
        copy.wait_recv()
    nearest = eh[j, 0] * has_low
    beyond = tb[0] * (rank > 1).astype(F32) + tb[1] * (rank > 2).astype(F32)
    prefix = (nearest + beyond)[1:2]
    low = nearest + beyond[1:2] * has_low
    high = (eh[j, 1] + (prefix + mine[1:2])) * has_high
    column = jnp.concatenate([jnp.broadcast_to(prefix, (128, ROWS))]).T
    v1 = v1 + jnp.concatenate([column, column], 1)
    phys[1] = to_time(v1)
    exchange(OUT[1], smoothed(v1, low, high) + coupled(1, 0))

    def stores(c):
        return pltpu.make_async_copy(stage.at[:, c], out.at[:, c], st_sem.at[c])

    def to_slots(c):
        xh, xl = split(arrived(OUT[c]))
        return (
            dot(xh, span_h[...], 0, 0) + dot(xl, span_h[...], 0, 0) + dot(xh, span_l[...], 0, 0)
        ) * (1.0 / 64)

    def put(c, x):
        stage[0, c] = x[:, :128]
        stage[1, c] = x[:, 128:]
        stores(c).start()

    u0 = to_slots(0)
    put(0, u0)
    w0 = to_slots(2)
    put(2, w0)
    slot = map_v[...]
    fi, ki = slot >> 6, slot & 63
    alpha = jnp.where(fi >= 32, fi - 64, fi).astype(F32) * (1.0 / 1024)
    beta = jnp.where(ki >= 32, ki - 64, ki).astype(F32) * (1.0 / 1024)
    source = jnp.concatenate(
        [
            alpha * u0[:, 128:] + beta * w0[:, 128:],
            -(alpha * u0[:, :128] + beta * w0[:, :128]),
        ],
        1,
    )
    sh, sl = split(source)
    running = dot(lower[...], sh) + dot(lower[...], sl)
    ft[...] = running[248:]
    finals = [
        pltpu.make_async_remote_copy(
            ft, ftb.at[o - 1], ft_sem.at[0, o - 1], ft_sem.at[1, o - 1],
            device_id=plane(o), device_id_type=MESH,
        )
        for o in (1, 2, 3)
    ]
    for copy in finals:
        copy.start()
    put(3, to_slots(3))
    put(4, to_slots(4))
    for copy in finals:
        copy.wait_recv()
    total = (
        ftb[0] * has_low + ftb[1] * (rank > 1).astype(F32) + ftb[2] * (rank > 2).astype(F32)
    )[7:8]
    running = running + total
    put(1, to_slots(1) + running)

    for c in range(5):
        stores(c).wait()
    send_fz.wait_send()
    wait_p.wait_send()
    for k in range(SLOTS):
        whole(k).wait_send()
    for j in range(10):
        for copy in edge_copies(j):
            copy.wait_send()
    for copy in totals + finals:
        copy.wait_send()


def solution(mesh):
    def on_device(adjoint, forward, mode_map):
        slots = mode_map.reshape(1, 128)
        consts = tables()
        vmem = pl.BlockSpec(memory_space=pltpu.VMEM)
        anywhere = pl.BlockSpec(memory_space=pl.ANY)
        return pl.pallas_call(
            kernel,
            out_shape=jax.ShapeDtypeStruct(adjoint.shape, F32),
            in_specs=[pl.BlockSpec(memory_space=pltpu.SMEM), vmem, anywhere, anywhere]
            + [vmem] * len(consts),
            out_specs=anywhere,
            scratch_shapes=[
                pltpu.VMEM((5, 2, ROWS, 128), F32),
                pltpu.VMEM((2, ROWS, 128), F32),
                pltpu.VMEM((2, ROWS, 128), F32),
                pltpu.VMEM((8, 128), jnp.int32),
                pltpu.VMEM((PEERS, 8, 128), jnp.int32),
                pltpu.VMEM((SLOTS, PEERS, 8, ROWS), F32),
                pltpu.VMEM((SLOTS, PEERS, 8, ROWS), F32),
                pltpu.VMEM((10, 2, 8, ROWS), F32),
                pltpu.VMEM((10, 2, 8, ROWS), F32),
                pltpu.VMEM((2, 8, ROWS), F32),
                pltpu.VMEM((8, ROWS), F32),
                pltpu.VMEM((3, 8, ROWS), F32),
                pltpu.VMEM((2, ROWS, ROWS), BF16),
                pltpu.VMEM((2, ROWS, ROWS), BF16),
                pltpu.VMEM((ROWS, 128), F32),
                pltpu.VMEM((7, ROWS, ROWS), F32),
                pltpu.VMEM((5, ROWS, ROWS), F32),
                pltpu.VMEM((2, 5, ROWS, 128), F32),
                pltpu.SemaphoreType.DMA((5,)),
                pltpu.SemaphoreType.DMA,
                pltpu.SemaphoreType.DMA((2,)),
                pltpu.SemaphoreType.DMA((2,)),
                pltpu.SemaphoreType.DMA((SLOTS,)),
                pltpu.SemaphoreType.DMA((SLOTS,)),
                pltpu.SemaphoreType.DMA((10, 2)),
                pltpu.SemaphoreType.DMA((10, 2)),
                pltpu.SemaphoreType.DMA((2, 2)),
                pltpu.SemaphoreType.DMA((2, 3)),
                pltpu.SemaphoreType.DMA((5,)),
            ],
            compiler_params=pltpu.CompilerParams(
                collective_id=0, has_side_effects=True, vmem_limit_bytes=48 << 20
            ),
        )(slots, slots, adjoint, forward, *consts)

    spec = P(None, None, ("wall", "ckpt"), "mode")
    return jax.shard_map(
        on_device,
        mesh=mesh,
        in_specs=(spec, P("ckpt", None, "wall", "mode"), P("mode")),
        out_specs=spec,
        check_vma=False,
    )
```

time: 551 us -> 74.4 us (0.14); the launches traced: 545 us -> 74 us
  local copies, waits for them, and re-layouts: 296 us -> 13.1 us
  matrix products: 87.6 us -> 0 us
  Pallas kernels: 0 us -> 60.9 us
  blocking collectives: 55.1 us -> 0 us
  starting transfers between devices: 46 us -> 0 us
  waiting for transfers between devices: 28.7 us -> 0 us
  other arithmetic: 16.9 us -> 0 us
  between operations: 14.4 us -> 0.02 us
    unnamed x49 -> x27, local copies, waits for them, and re-layouts: 153 us -> 13.1 us
    dot_general x42 -> x0, matrix products: 87.6 us -> none  [the longest x5 15.8 us: span_dft(): jnp.einsum('...k,kz->...z', imag_part, sine_part, precision=HIGHEST)]
    pallas_call x0 -> x1, Pallas kernels: none -> 60.9 us  [on_device(): pl.pallas_call(kernel, out_shape=jax.ShapeDtypeStruct(adjoint.shape, F32)...]
    all_gather x3 -> x0, blocking collectives: 55.1 us -> none  [the longest x1 40 us: on_device(): full_map = lax.all_gather(mode_map, 'mode', axis=0, tiled=True)]
    all_to_all x6 -> x0, local copies, waits for them, and re-layouts: 45.6 us -> none  [the longest x3 43.7 us: to_modes(): lax.all_to_all(values, 'mode', split_axis=3, concat_axis=2, tiled=True)]
    div x2 -> x0, local copies, waits for them, and re-layouts: 35.7 us -> none  [coupling_term(): return jnp.stack([real_part, imag_part]) / (NF * NK)]
    all_to_all x5 -> x0, starting transfers between devices: 31.8 us -> none  [the longest x2 11.4 us: to_modes(): lax.all_to_all(values, 'mode', split_axis=3, concat_axis=2, tiled=True)]
    all_to_all x5 -> x0, waiting for transfers between devices: 28 us -> none  [the longest x2 17.4 us: to_modes(): lax.all_to_all(values, 'mode', split_axis=3, concat_axis=2, tiled=True)]
  transfers between devices with their start and end apart: 10 -> 0, of which waited for: 3 -> 0; matrix products, arithmetic and copies ran while one was open for 9% -> 0% of each run, Pallas kernels for 0% -> 0%
where the time goes in v1:
time: 74.4 us; the launch traced here: 74 us
  Pallas kernels  60.9 us (82%)
  local copies, waits for them, and re-layouts  13.1 us (18%)
    pallas_call x1, Pallas kernels, on_device(): pl.pallas_call(kernel, out_shape=jax.ShapeDtypeStruct(adjoint.shape, F32)...  60.9 us
    unnamed x27, local copies, waits for them, and re-layouts  13.1 us

profile of v1, /device:TPU:1, one launch (start us, length us, event | category | flops | bytes accessed | tf_op | source)
XLA Modules:
  0.0 74.0 jit_solution(6601477247999551655)
XLA Ops:
  0.0 0.0 copy-start
  0.0 1.3 %copy-done = f32[2,5,256,128]{3,2,1,0:T(8,128)S(1)} copy-done((f32[2,5,256,128]{3,2,1,0:T(8,128)S(1)}, f32[2,5,256,128]{3,2,1,0:T(8,128)}, u32[]{:S(2)}) %copy-start) | copy-done | bytes 1310744
  1.3 0.0 copy-start.1
  1.3 1.0 %copy-done.1 = f32[1,2,512,128]{3,2,1,0:T(8,128)S(1)} copy-done((f32[1,2,512,128]{3,2,1,0:T(8,128)S(1)}, f32[1,2,512,128]{3,2,1,0:T(8,128)}, u32[]{:S(2)}) %copy-start.1) | copy-done | bytes 524312
  2.4 0.0 copy-start.2
  2.4 0.9 %copy-done.2 = bf16[256,256]{1,0:T(8,128)(2,1)S(1)} copy-done((bf16[256,256]{1,0:T(8,128)(2,1)S(1)}, bf16[256,256]{1,0:T(8,128)(2,1)}, u32[]{:S(2)}) %copy-start.2) | copy-done | bytes 131096
  3.3 0.0 copy-start.3
  3.3 0.9 %copy-done.3 = bf16[256,256]{1,0:T(8,128)(2,1)S(1)} copy-done((bf16[256,256]{1,0:T(8,128)(2,1)S(1)}, bf16[256,256]{1,0:T(8,128)(2,1)}, u32[]{:S(2)}) %copy-start.3) | copy-done | bytes 131096
  4.2 0.0 copy-start.4
  4.2 0.9 %copy-done.4 = bf16[256,256]{1,0:T(8,128)(2,1)S(1)} copy-done((bf16[256,256]{1,0:T(8,128)(2,1)S(1)}, bf16[256,256]{1,0:T(8,128)(2,1)}, u32[]{:S(2)}) %copy-start.4) | copy-done | bytes 131096
  5.1 0.0 copy-start.5
  5.1 0.9 %copy-done.5 = bf16[256,256]{1,0:T(8,128)(2,1)S(1)} copy-done((bf16[256,256]{1,0:T(8,128)(2,1)S(1)}, bf16[256,256]{1,0:T(8,128)(2,1)}, u32[]{:S(2)}) %copy-start.5) | copy-done | bytes 131096
  6.0 0.0 copy-start.6
  6.0 0.9 %copy-done.6 = bf16[256,256]{1,0:T(8,128)(2,1)S(1)} copy-done((bf16[256,256]{1,0:T(8,128)(2,1)S(1)}, bf16[256,256]{1,0:T(8,128)(2,1)}, u32[]{:S(2)}) %copy-start.6) | copy-done | bytes 131096
  6.9 0.0 copy-start.7
  6.9 0.9 %copy-done.7 = bf16[256,256]{1,0:T(8,128)(2,1)S(1)} copy-done((bf16[256,256]{1,0:T(8,128)(2,1)S(1)}, bf16[256,256]{1,0:T(8,128)(2,1)}, u32[]{:S(2)}) %copy-start.7) | copy-done | bytes 131096
  7.8 0.0 copy-start.8
  7.8 0.9 %copy-done.8 = bf16[256,256]{1,0:T(8,128)(2,1)S(1)} copy-done((bf16[256,256]{1,0:T(8,128)(2,1)S(1)}, bf16[256,256]{1,0:T(8,128)(2,1)}, u32[]{:S(2)}) %copy-start.8) | copy-done | bytes 131096
  8.7 0.0 copy-start.9
  8.7 0.9 %copy-done.9 = bf16[256,256]{1,0:T(8,128)(2,1)S(1)} copy-done((bf16[256,256]{1,0:T(8,128)(2,1)S(1)}, bf16[256,256]{1,0:T(8,128)(2,1)}, u32[]{:S(2)}) %copy-start.9) | copy-done | bytes 131096
  9.6 0.0 copy-start.10
  9.6 0.9 %copy-done.10 = bf16[256,256]{1,0:T(8,128)(2,1)S(1)} copy-done((bf16[256,256]{1,0:T(8,128)(2,1)S(1)}, bf16[256,256]{1,0:T(8,128)(2,1)}, u32[]{:S(2)}) %copy-start.10) | copy-done | bytes 131096
  10.5 0.0 copy-start.11
  10.5 0.9 %copy-done.11 = bf16[256,256]{1,0:T(8,128)(2,1)S(1)} copy-done((bf16[256,256]{1,0:T(8,128)(2,1)S(1)}, bf16[256,256]{1,0:T(8,128)(2,1)}, u32[]{:S(2)}) %copy-start.11) | copy-done | bytes 131096
  11.4 0.0 copy-start.12
  11.4 0.7 copy-done.12
  12.1 60.9 %shard_map.127 = f32[2,5,256,128]{3,2,1,0:T(8,128)S(1)} custom-call(s32[1,128]{1,0:T(1,128)S(1)} %bitcast.1, s32[1,128]{1,0:T(1,128)S(1)} %bitcast.2, f32[2,5,256,128]{3,2,1,0:T(8,128)S(1)} %copy-done, f32[1,2,512,128]{3,2,1,0:T(8,128)S(1)} %copy-done.1, bf16[256,256]{1,0:T(8,128)(2,1)S(1)} %copy-done.11, bf16[256,256]{1,0:T(8,128)(2,1)S(1)} %copy-done.10, ...), custom_call_target="tpu_custom_call" | custom-call | tf_op jit(solution)/shard_map/pallas_call | solution.py:405
  73.0 1.1 %copy.15 = f32[2,5,256,128]{3,2,1,0:T(8,128)} copy(f32[2,5,256,128]{3,2,1,0:T(8,128)S(1)} %shard_map.127) | data formatting | bytes 2621440
Async XLA Ops:
  0.0 1.3 %copy-start = (f32[2,5,256,128]{3,2,1,0:T(8,128)S(1)}, f32[2,5,256,128]{3,2,1,0:T(8,128)}, u32[]{:S(2)}) copy-start(f32[2,5,256,128]{3,2,1,0:T(8,128)} %adj.1) | copy-start | bytes 3932164
  1.3 1.0 %copy-start.1 = (f32[1,2,512,128]{3,2,1,0:T(8,128)S(1)}, f32[1,2,512,128]{3,2,1,0:T(8,128)}, u32[]{:S(2)}) copy-start(f32[1,2,512,128]{3,2,1,0:T(8,128)} %fwd.1) | copy-start | bytes 1572868
  2.4 0.9 %copy-start.2 = (bf16[256,256]{1,0:T(8,128)(2,1)S(1)}, bf16[256,256]{1,0:T(8,128)(2,1)}, u32[]{:S(2)}) copy-start(bf16[256,256]{1,0:T(8,128)(2,1)} %constant.29.clone.lower) | copy-start | bytes 393220
  3.3 0.9 %copy-start.3 = (bf16[256,256]{1,0:T(8,128)(2,1)S(1)}, bf16[256,256]{1,0:T(8,128)(2,1)}, u32[]{:S(2)}) copy-start(bf16[256,256]{1,0:T(8,128)(2,1)} %constant.28.clone.upper) | copy-start | bytes 393220
  4.2 0.9 %copy-start.4 = (bf16[256,256]{1,0:T(8,128)(2,1)S(1)}, bf16[256,256]{1,0:T(8,128)(2,1)}, u32[]{:S(2)}) copy-start(bf16[256,256]{1,0:T(8,128)(2,1)} %constant.27.clone.der_l) | copy-start | bytes 393220
  5.1 0.9 %copy-start.5 = (bf16[256,256]{1,0:T(8,128)(2,1)S(1)}, bf16[256,256]{1,0:T(8,128)(2,1)}, u32[]{:S(2)}) copy-start(bf16[256,256]{1,0:T(8,128)(2,1)} %constant.26.clone.der_h) | copy-start | bytes 393220
  6.0 0.9 %copy-start.6 = (bf16[256,256]{1,0:T(8,128)(2,1)S(1)}, bf16[256,256]{1,0:T(8,128)(2,1)}, u32[]{:S(2)}) copy-start(bf16[256,256]{1,0:T(8,128)(2,1)} %constant.25.clone.inv_l) | copy-start | bytes 393220
  6.9 0.9 %copy-start.7 = (bf16[256,256]{1,0:T(8,128)(2,1)S(1)}, bf16[256,256]{1,0:T(8,128)(2,1)}, u32[]{:S(2)}) copy-start(bf16[256,256]{1,0:T(8,128)(2,1)} %constant.24.clone.inv_h) | copy-start | bytes 393220
  7.8 0.9 %copy-start.8 = (bf16[256,256]{1,0:T(8,128)(2,1)S(1)}, bf16[256,256]{1,0:T(8,128)(2,1)}, u32[]{:S(2)}) copy-start(bf16[256,256]{1,0:T(8,128)(2,1)} %constant.23.clone.time_l) | copy-start | bytes 393220
  8.7 0.9 %copy-start.9 = (bf16[256,256]{1,0:T(8,128)(2,1)S(1)}, bf16[256,256]{1,0:T(8,128)(2,1)}, u32[]{:S(2)}) copy-start(bf16[256,256]{1,0:T(8,128)(2,1)} %constant.22.clone.time_h) | copy-start | bytes 393220
  9.6 0.9 %copy-start.10 = (bf16[256,256]{1,0:T(8,128)(2,1)S(1)}, bf16[256,256]{1,0:T(8,128)(2,1)}, u32[]{:S(2)}) copy-start(bf16[256,256]{1,0:T(8,128)(2,1)} %constant.21.clone.span_l) | copy-start | bytes 393220
  10.5 0.9 %copy-start.11 = (bf16[256,256]{1,0:T(8,128)(2,1)S(1)}, bf16[256,256]{1,0:T(8,128)(2,1)}, u32[]{:S(2)}) copy-start(bf16[256,256]{1,0:T(8,128)(2,1)} %constant.20.clone.span_h) | copy-start | bytes 393220
  11.4 0.7 copy-start.12

commit v2 on v1

--- a/solution.py
+++ b/solution.py
@@ -17,8 +17,8 @@
 BF16 = jnp.bfloat16
 MESH = pl.DeviceIdType.MESH
 
-IN = {2: 0, 0: 1, 3: 3, 4: 5, 1: 6}
-F_OWN, F_OTHER, MID, BACK = 2, 4, 7, 8
+IN = {2: 0, 0: 1, 3: 4, 1: 5, 4: 6}
+F_OWN, F_OTHER, MID, BACK = 2, 3, 7, 8
 OUT = {0: 9, 2: 10, 3: 11, 4: 12, 1: 13}
 SLOTS = 14
 
@@ -26,7 +26,7 @@
 def hi_lo(table):
     hi = table.astype(np.float32).astype(BF16)
     lo = (table - hi.astype(np.float64)).astype(np.float32).astype(BF16)
-    return jnp.asarray(hi), jnp.asarray(lo)
+    return hi, lo
 
 
 def complex_blocks(cosine, sine):
@@ -50,13 +50,17 @@
         "pqzx,ab->zpaxqb", complex_blocks(slope.real, slope.imag), eye
     ).reshape(256, 256)
     upto = (np.arange(256)[:, None] <= np.arange(256)[None, :]).astype(np.float32)
-    return (
-        *hi_lo(span),
-        *hi_lo(time),
-        *hi_lo(-time.T / 128),
-        *hi_lo(deriv),
-        jnp.asarray(upto.astype(BF16)),
-        jnp.asarray(upto.T.astype(BF16)),
+    return jnp.asarray(
+        np.stack(
+            [
+                *hi_lo(span),
+                *hi_lo(time),
+                *hi_lo(-time.T / 128),
+                *hi_lo(deriv),
+                upto.astype(BF16),
+                upto.T.astype(BF16),
+            ]
+        )
     )
 
 
@@ -70,18 +74,21 @@
 
 
 def kernel(
-    map_s, map_v, adj, fwd, span_h, span_l, time_h, time_l, inv_h, inv_l, der_h, der_l,
-    upper, lower, out,
-    xin, fin, fz, ptile, ptab, sb, db, es, eh, tb, ft, ftb, tm, ti, amp, phys, qs, stage,
-    load_sem, fload_sem, fz_sem, p_sem, ssem, rsem, es_sem, er_sem, tt_sem, ft_sem, st_sem,
+    slots, adj, fwd, consts, out,
+    map_v, table, xin, fin, fz, ptab, sb, db, es, eh, tb, ft, ftb, tm, ti, amp, phys, qs, stage,
+    map_sem, table_sem, load_sem, fload_sem, fz_sem, p_sem, ssem, rsem, es_sem, er_sem, tt_sem, ft_sem, st_sem,
 ):
     me = lax.axis_index("mode")
     wall, ckpt = lax.axis_index("wall"), lax.axis_index("ckpt")
     mx, my, mc = me // 8, (me // 2) % 4, me % 2
     rank = wall * 2 + ckpt
 
-    def peer(i):
-        return ((mx + i // 8) % 4) * 8 + ((my + (i // 2) % 4) % 4) * 2 + (mc + i % 2) % 2
+    at_x = [((mx + a) % 4) * 8 for a in range(4)]
+    at_y = [((my + b) % 4) * 2 for b in range(4)]
+    at_c = [mc, 1 - mc]
+    peers = [
+        at_x[a] + at_y[b] + at_c[c] for a in range(4) for b in range(4) for c in range(2)
+    ][1:]
 
     def plane(offset):
         other = (rank + offset) % 4
@@ -89,64 +96,50 @@
 
     bar = pltpu.get_barrier_semaphore()
 
-    def greet(i, carry):
-        pl.semaphore_signal(bar, inc=1, device_id={"mode": peer(i)}, device_id_type=MESH)
-        return carry
-
-    lax.fori_loop(1, PEERS, greet, 0)
+    for p in peers:
+        pl.semaphore_signal(bar, inc=1, device_id={"mode": p}, device_id_type=MESH)
     for o in (1, 2, 3):
         pl.semaphore_signal(bar, inc=1, device_id=plane(o), device_id_type=MESH)
 
+    load_table = [
+        pltpu.make_async_copy(consts.at[rows], table.at[rows], table_sem.at[i])
+        for i, rows in enumerate((pl.ds(0, 2), pl.ds(2, 8)))
+    ]
+    load_table[0].start()
+    span_h, span_l, time_h, time_l, inv_h, inv_l, der_h, der_l, upper, lower = (
+        table.at[i] for i in range(10)
+    )
+
+    load_map = pltpu.make_async_copy(slots, map_v, map_sem)
     loads = {}
     for c in (2, 0, 3, 4, 1):
         loads[c] = pltpu.make_async_copy(adj.at[:, c], xin.at[c], load_sem.at[c])
         loads[c].start()
+        if c == 2:
+            load_map.start()
     load_f = pltpu.make_async_copy(
         fwd.at[0, :, pl.ds(ckpt * ROWS, ROWS)], fin, fload_sem
     )
     load_f.start()
-
-    row8 = lax.broadcasted_iota(jnp.int32, (8, 128), 0)
-    ptile[...] = jnp.where(row8 % 2 == 0, map_s[0, 0] >> 6, map_s[0, 64] >> 6)
-
-    pl.semaphore_wait(bar, PEERS - 1 + 3)
-
-    send_fz = pltpu.make_async_remote_copy(
-        fwd.at[0, :, pl.ds((1 - ckpt) * ROWS, ROWS)], fz, fz_sem.at[0], fz_sem.at[1],
-        device_id={"ckpt": 1 - ckpt}, device_id_type=MESH,
-    )
-    send_fz.start()
-
-    def send_p(i, carry):
-        p = peer(i)
-        pltpu.make_async_remote_copy(
-            ptile, ptab.at[me], p_sem.at[0], p_sem.at[1],
-            device_id={"mode": p}, device_id_type=MESH,
-        ).start()
-        return carry
-
-    lax.fori_loop(1, PEERS, send_p, 0)
-    ptab[me] = ptile[...]
+    load_table[1].start()
 
     def exchange(k, value):
         sb[k] = value.reshape(PEERS, 8, ROWS)
-
-        def one(i, carry):
-            p = peer(i)
+        send(k)
+
+    def send(k):
+        for p in peers:
             pltpu.make_async_remote_copy(
                 sb.at[k, p], db.at[k, me], ssem.at[k], rsem.at[k],
                 device_id={"mode": p}, device_id_type=MESH,
             ).start()
-            return carry
-
-        lax.fori_loop(1, PEERS, one, 0)
         db[k, me] = sb[k, me]
 
     def whole(k):
         n = pl.ds(0, PEERS - 1)
         return pltpu.make_async_remote_copy(
             sb.at[k, n], db.at[k, n], ssem.at[k], rsem.at[k],
-            device_id={"mode": peer(1)}, device_id_type=MESH,
+            device_id={"mode": peers[0]}, device_id_type=MESH,
         )
 
     def arrived(k):
@@ -164,7 +157,25 @@
         loads[c].wait()
         exchange(IN[c], to_span(xin[c, 0], xin[c, 1]))
 
-    send_field(2)
+    load_table[0].wait()
+    loads[2].wait()
+    sb[IN[2]] = to_span(xin[2, 0], xin[2, 1]).reshape(PEERS, 8, ROWS)
+    load_map.wait()
+
+    pl.semaphore_wait(bar, PEERS - 1 + 3)
+
+    send_fz = pltpu.make_async_remote_copy(
+        fwd.at[0, :, pl.ds((1 - ckpt) * ROWS, ROWS)], fz, fz_sem.at[0], fz_sem.at[1],
+        device_id={"ckpt": 1 - ckpt}, device_id_type=MESH,
+    )
+    send_fz.start()
+    send(IN[2])
+    for p in peers:
+        pltpu.make_async_remote_copy(
+            map_v, ptab.at[me], p_sem.at[0], p_sem.at[1],
+            device_id={"mode": p}, device_id_type=MESH,
+        ).start()
+    ptab[me] = map_v[...]
     send_field(0)
     load_f.wait()
     exchange(F_OWN, to_span(fin[0], fin[1]))
@@ -173,12 +184,14 @@
     n = pl.ds(0, PEERS - 1)
     wait_p = pltpu.make_async_remote_copy(
         ptab.at[n], ptab.at[n], p_sem.at[0], p_sem.at[1],
-        device_id={"mode": peer(1)}, device_id_type=MESH,
+        device_id={"mode": peers[0]}, device_id_type=MESH,
     )
     wait_p.wait_recv()
-    freq = ptab[...].reshape(ROWS, 128)
+    load_table[1].wait()
     row = lax.broadcasted_iota(jnp.int32, (ROWS, 128), 0)
     lane = lax.broadcasted_iota(jnp.int32, (ROWS, 128), 1)
+    held = jnp.broadcast_to(ptab[...], (PEERS, 8, 128)).reshape(ROWS, 128) >> 6
+    freq = jnp.where(row % 2 == lane // 64, held, pltpu.roll(held, 64, 1))
     inside = (row % 8) // 2
     onehot = jnp.concatenate(
         [
@@ -263,28 +276,27 @@
     begin(0)
     send_fz.wait_recv()
     exchange(F_OTHER, to_span(fz[0], fz[1]))
-    send_field(4)
     send_field(1)
     phys[5 + ckpt] = to_time(arrived(F_OWN))
-    begin(3)
     phys[6 - ckpt] = to_time(arrived(F_OTHER))
     first_step(2)
     exchange(MID, qs[2])
+    send_field(4)
     first_step(0)
     again(0)
     again(2)
-    begin(4)
+    begin(3)
+    begin(1)
     finish(0)
     first_step(3)
     again(3)
+    exchange(BACK, dot3(der_h, der_l, arrived(MID)))
     finish(2)
-    exchange(BACK, dot3(der_h, der_l, arrived(MID)))
+    first_step(1)
+    begin(4)
+    finish(3)
     first_step(4)
     again(4)
-    begin(1)
-    first_step(1)
-    finish(3)
-    finish(4)
 
     u1 = qs[0]
     row2 = lax.broadcasted_iota(jnp.int32, (ROWS, ROWS), 0)
@@ -320,6 +332,7 @@
     for copy in totals:
         copy.start()
     mine = comb[:8]
+    finish(4)
     for copy in edge_copies(j) + totals:
         copy.wait_recv()
     nearest = eh[j, 0] * has_low
@@ -374,13 +387,13 @@
     for copy in finals:
         copy.start()
     put(3, to_slots(3))
-    put(4, to_slots(4))
     for copy in finals:
         copy.wait_recv()
     total = (
         ftb[0] * has_low + ftb[1] * (rank > 1).astype(F32) + ftb[2] * (rank > 2).astype(F32)
     )[7:8]
     running = running + total
+    put(4, to_slots(4))
     put(1, to_slots(1) + running)
 
     for c in range(5):
@@ -400,20 +413,19 @@
     def on_device(adjoint, forward, mode_map):
         slots = mode_map.reshape(1, 128)
         consts = tables()
-        vmem = pl.BlockSpec(memory_space=pltpu.VMEM)
         anywhere = pl.BlockSpec(memory_space=pl.ANY)
         return pl.pallas_call(
             kernel,
             out_shape=jax.ShapeDtypeStruct(adjoint.shape, F32),
-            in_specs=[pl.BlockSpec(memory_space=pltpu.SMEM), vmem, anywhere, anywhere]
-            + [vmem] * len(consts),
+            in_specs=[pl.BlockSpec(memory_space=pltpu.HBM)] * 4,
             out_specs=anywhere,
             scratch_shapes=[
+                pltpu.VMEM((1, 128), jnp.int32),
+                pltpu.VMEM((10, ROWS, ROWS), BF16),
                 pltpu.VMEM((5, 2, ROWS, 128), F32),
                 pltpu.VMEM((2, ROWS, 128), F32),
                 pltpu.VMEM((2, ROWS, 128), F32),
-                pltpu.VMEM((8, 128), jnp.int32),
-                pltpu.VMEM((PEERS, 8, 128), jnp.int32),
+                pltpu.VMEM((PEERS, 1, 128), jnp.int32),
                 pltpu.VMEM((SLOTS, PEERS, 8, ROWS), F32),
                 pltpu.VMEM((SLOTS, PEERS, 8, ROWS), F32),
                 pltpu.VMEM((10, 2, 8, ROWS), F32),
@@ -427,6 +439,8 @@
                 pltpu.VMEM((7, ROWS, ROWS), F32),
                 pltpu.VMEM((5, ROWS, ROWS), F32),
                 pltpu.VMEM((2, 5, ROWS, 128), F32),
+                pltpu.SemaphoreType.DMA,
+                pltpu.SemaphoreType.DMA((2,)),
                 pltpu.SemaphoreType.DMA((5,)),
                 pltpu.SemaphoreType.DMA,
                 pltpu.SemaphoreType.DMA((2,)),
@@ -440,9 +454,9 @@
                 pltpu.SemaphoreType.DMA((5,)),
             ],
             compiler_params=pltpu.CompilerParams(
-                collective_id=0, has_side_effects=True, vmem_limit_bytes=48 << 20
+                collective_id=0, has_side_effects=True, vmem_limit_bytes=53400 << 10
             ),
-        )(slots, slots, adjoint, forward, *consts)
+        )(slots, adjoint, forward, consts)
 
     spec = P(None, None, ("wall", "ckpt"), "mode")
     return jax.shard_map(

time: 74.4 us -> 58.6 us (0.79)
  local copies, waits for them, and re-layouts: 13.1 us -> 2.75 us
  Pallas kernels: 60.9 us -> 55.6 us
    unnamed x27 -> x5, local copies, waits for them, and re-layouts: 13.1 us -> 2.75 us
    pallas_call x1, Pallas kernels: 60.9 us -> 55.6 us  [on_device(): pl.pallas_call(kernel, out_shape=jax.ShapeDtypeStruct(adjoint.shape, F32)...]
where the time goes in v2:
time: 58.6 us; the launch traced here: 58.4 us
  Pallas kernels  55.6 us (95%)
  local copies, waits for them, and re-layouts  2.75 us (5%)
    pallas_call x1, Pallas kernels, on_device(): pl.pallas_call(kernel, out_shape=jax.ShapeDtypeStruct(adjoint.shape, F32)...  55.6 us
    unnamed x5, local copies, waits for them, and re-layouts  2.75 us

profile of v2, /device:TPU:1, one launch (start us, length us, event | category | flops | bytes accessed | tf_op | source)
XLA Modules:
  0.0 58.4 jit_solution(561245745919449315)
XLA Ops:
  0.0 0.0 copy-start
  0.0 1.0 %copy-done = f32[1,2,512,128]{3,2,1,0:T(8,128)S(1)} copy-done((f32[1,2,512,128]{3,2,1,0:T(8,128)S(1)}, f32[1,2,512,128]{3,2,1,0:T(8,128)}, u32[]{:S(2)}) %copy-start) | copy-done | bytes 524312
  1.0 0.0 copy-start.1
  1.0 0.7 %copy-done.1 = s32[128]{0:T(128)S(1)} copy-done((s32[128]{0:T(128)S(1)}, s32[128]{0:T(128)}, u32[]{:S(2)}) %copy-start.1) | copy-done | bytes 536
  1.7 55.6 %shard_map.46 = f32[2,5,256,128]{3,2,1,0:T(8,128)S(1)} custom-call(s32[1,128]{1,0:T(1,128)S(1)} %bitcast.1, f32[2,5,256,128]{3,2,1,0:T(8,128)} %adj.1, f32[1,2,512,128]{3,2,1,0:T(8,128)S(1)} %copy-done, bf16[10,256,256]{2,1,0:T(8,128)(2,1)} %constant.2.clone.consts), custom_call_target="tpu_custom_call" | custom-call | tf_op jit(solution)/shard_map/pallas_call | solution.py:417
  57.3 1.1 %copy.6 = f32[2,5,256,128]{3,2,1,0:T(8,128)} copy(f32[2,5,256,128]{3,2,1,0:T(8,128)S(1)} %shard_map.46) | data formatting | bytes 2621440
Async XLA Ops:
  0.0 1.0 %copy-start = (f32[1,2,512,128]{3,2,1,0:T(8,128)S(1)}, f32[1,2,512,128]{3,2,1,0:T(8,128)}, u32[]{:S(2)}) copy-start(f32[1,2,512,128]{3,2,1,0:T(8,128)} %fwd.1) | copy-start | bytes 1572868
  1.0 0.7 %copy-start.1 = (s32[128]{0:T(128)S(1)}, s32[128]{0:T(128)}, u32[]{:S(2)}) copy-start(s32[128]{0:T(128)} %param.6) | copy-start | bytes 1540

commit v3 on v2

--- a/solution.py
+++ b/solution.py
@@ -75,8 +75,8 @@
 
 def kernel(
     slots, adj, fwd, consts, out,
-    map_v, table, xin, fin, fz, ptab, sb, db, es, eh, tb, ft, ftb, tm, ti, amp, phys, qs, stage,
-    map_sem, table_sem, load_sem, fload_sem, fz_sem, p_sem, ssem, rsem, es_sem, er_sem, tt_sem, ft_sem, st_sem,
+    map_v, table, xin, fin, fz, ptab, sb, db, es, eh, tb, ft, ftb, tm, ti, amp, phys, qs,
+    map_sem, table_sem, load_sem, fload_sem, fz_sem, p_sem, ssem, rsem, es_sem, er_sem, tt_sem, ft_sem,
 ):
     me = lax.axis_index("mode")
     wall, ckpt = lax.axis_index("wall"), lax.axis_index("ckpt")
@@ -277,11 +277,11 @@
     send_fz.wait_recv()
     exchange(F_OTHER, to_span(fz[0], fz[1]))
     send_field(1)
+    send_field(4)
     phys[5 + ckpt] = to_time(arrived(F_OWN))
     phys[6 - ckpt] = to_time(arrived(F_OTHER))
     first_step(2)
     exchange(MID, qs[2])
-    send_field(4)
     first_step(0)
     again(0)
     again(2)
@@ -345,9 +345,6 @@
     phys[1] = to_time(v1)
     exchange(OUT[1], smoothed(v1, low, high) + coupled(1, 0))
 
-    def stores(c):
-        return pltpu.make_async_copy(stage.at[:, c], out.at[:, c], st_sem.at[c])
-
     def to_slots(c):
         xh, xl = split(arrived(OUT[c]))
         return (
@@ -355,9 +352,8 @@
         ) * (1.0 / 64)
 
     def put(c, x):
-        stage[0, c] = x[:, :128]
-        stage[1, c] = x[:, 128:]
-        stores(c).start()
+        out[0, c] = x[:, :128]
+        out[1, c] = x[:, 128:]
 
     u0 = to_slots(0)
     put(0, u0)
@@ -396,8 +392,6 @@
     put(4, to_slots(4))
     put(1, to_slots(1) + running)
 
-    for c in range(5):
-        stores(c).wait()
     send_fz.wait_send()
     wait_p.wait_send()
     for k in range(SLOTS):
@@ -413,12 +407,11 @@
     def on_device(adjoint, forward, mode_map):
         slots = mode_map.reshape(1, 128)
         consts = tables()
-        anywhere = pl.BlockSpec(memory_space=pl.ANY)
         return pl.pallas_call(
             kernel,
             out_shape=jax.ShapeDtypeStruct(adjoint.shape, F32),
             in_specs=[pl.BlockSpec(memory_space=pltpu.HBM)] * 4,
-            out_specs=anywhere,
+            out_specs=pl.BlockSpec(memory_space=pltpu.VMEM),
             scratch_shapes=[
                 pltpu.VMEM((1, 128), jnp.int32),
                 pltpu.VMEM((10, ROWS, ROWS), BF16),
@@ -438,7 +431,6 @@
                 pltpu.VMEM((ROWS, 128), F32),
                 pltpu.VMEM((7, ROWS, ROWS), F32),
                 pltpu.VMEM((5, ROWS, ROWS), F32),
-                pltpu.VMEM((2, 5, ROWS, 128), F32),
                 pltpu.SemaphoreType.DMA,
                 pltpu.SemaphoreType.DMA((2,)),
                 pltpu.SemaphoreType.DMA((5,)),
@@ -451,12 +443,11 @@
                 pltpu.SemaphoreType.DMA((10, 2)),
                 pltpu.SemaphoreType.DMA((2, 2)),
                 pltpu.SemaphoreType.DMA((2, 3)),
-                pltpu.SemaphoreType.DMA((5,)),
             ],
             compiler_params=pltpu.CompilerParams(
-                collective_id=0, has_side_effects=True, vmem_limit_bytes=53400 << 10
+                collective_id=0, has_side_effects=True, vmem_limit_bytes=48 << 20
             ),
-        )(slots, adjoint, forward, consts)
+        )(*(pltpu.with_memory_space_constraint(x, pltpu.HBM) for x in (slots, adjoint, forward, consts)))
 
     spec = P(None, None, ("wall", "ckpt"), "mode")
     return jax.shard_map(

time: 58.6 us -> 56.2 us (0.959)
  local copies, waits for them, and re-layouts: 2.75 us -> 1.06 us
  Pallas kernels: 55.6 us -> 55 us
    unnamed x5 -> x1, local copies, waits for them, and re-layouts: 2.75 us -> 1.06 us
    pallas_call x1, Pallas kernels: 55.6 us -> 55 us  [on_device(): pl.pallas_call(kernel, out_shape=jax.ShapeDtypeStruct(adjoint.shape, F32)...]
where the time goes in v3:
time: 56.2 us; the launch traced here: 56 us
  Pallas kernels  55 us (98%)
  local copies, waits for them, and re-layouts  1.06 us (2%)
    pallas_call x1, Pallas kernels, on_device(): pl.pallas_call(kernel, out_shape=jax.ShapeDtypeStruct(adjoint.shape, F32)...  55 us

profile of v3, /device:TPU:1, one launch (start us, length us, event | category | flops | bytes accessed | tf_op | source)
XLA Modules:
  0.0 56.0 jit_solution(12019713713984771033)
XLA Ops:
  0.0 55.0 %shard_map.46 = f32[2,5,256,128]{3,2,1,0:T(8,128)S(1)} custom-call(s32[1,128]{1,0:T(1,128)} %bitcast.1, f32[2,5,256,128]{3,2,1,0:T(8,128)} %adj.1, f32[1,2,512,128]{3,2,1,0:T(8,128)} %fwd.1, bf16[10,256,256]{2,1,0:T(8,128)(2,1)} %constant.2.clone.consts), custom_call_target="tpu_custom_call" | custom-call | tf_op jit(solution)/shard_map/pallas_call | solution.py:410
  55.0 1.1 %copy.6 = f32[2,5,256,128]{3,2,1,0:T(8,128)} copy(f32[2,5,256,128]{3,2,1,0:T(8,128)S(1)} %shard_map.46) | data formatting | bytes 2621440

commit v4 on v3

--- a/solution.py
+++ b/solution.py
@@ -86,9 +86,9 @@
     at_x = [((mx + a) % 4) * 8 for a in range(4)]
     at_y = [((my + b) % 4) * 2 for b in range(4)]
     at_c = [mc, 1 - mc]
-    peers = [
-        at_x[a] + at_y[b] + at_c[c] for a in range(4) for b in range(4) for c in range(2)
-    ][1:]
+    steps = [(a, b, c) for a in range(4) for b in range(4) for c in range(2)][1:]
+    steps.sort(key=lambda t: -min(t[0], 4 - t[0]) - min(t[1], 4 - t[1]))
+    peers = [at_x[a] + at_y[b] + at_c[c] for a, b, c in steps]
 
     def plane(offset):
         other = (rank + offset) % 4

time: 56.2 us -> 54.2 us (0.964)
  Pallas kernels: 55 us -> 53 us
    pallas_call x1, Pallas kernels: 55 us -> 53 us  [on_device(): pl.pallas_call(kernel, out_shape=jax.ShapeDtypeStruct(adjoint.shape, F32)...]
where the time goes in v4:
time: 54.2 us; the launch traced here: 54.1 us
  Pallas kernels  53 us (98%)
  local copies, waits for them, and re-layouts  1.06 us (2%)
    pallas_call x1, Pallas kernels, on_device(): pl.pallas_call(kernel, out_shape=jax.ShapeDtypeStruct(adjoint.shape, F32)...  53 us

profile of v4, /device:TPU:1, one launch (start us, length us, event | category | flops | bytes accessed | tf_op | source)
XLA Modules:
  0.0 54.1 jit_solution(12721893137432779596)
XLA Ops:
  0.0 53.0 %shard_map.46 = f32[2,5,256,128]{3,2,1,0:T(8,128)S(1)} custom-call(s32[1,128]{1,0:T(1,128)} %bitcast.1, f32[2,5,256,128]{3,2,1,0:T(8,128)} %adj.1, f32[1,2,512,128]{3,2,1,0:T(8,128)} %fwd.1, bf16[10,256,256]{2,1,0:T(8,128)(2,1)} %constant.2.clone.consts), custom_call_target="tpu_custom_call" | custom-call | tf_op jit(solution)/shard_map/pallas_call | solution.py:410
  53.0 1.1 %copy.6 = f32[2,5,256,128]{3,2,1,0:T(8,128)} copy(f32[2,5,256,128]{3,2,1,0:T(8,128)S(1)} %shard_map.46) | data formatting | bytes 2621440

commit v5 on v4

--- a/solution.py
+++ b/solution.py
@@ -280,10 +280,10 @@
     send_field(4)
     phys[5 + ckpt] = to_time(arrived(F_OWN))
     phys[6 - ckpt] = to_time(arrived(F_OTHER))
+    first_step(0)
+    again(0)
     first_step(2)
     exchange(MID, qs[2])
-    first_step(0)
-    again(0)
     again(2)
     begin(3)
     begin(1)

time: 54.2 us -> 54 us (level)
  no operation moved by 1% of the time
where the time goes in v5:
time: 54 us; the launch traced here: 53.9 us
  Pallas kernels  52.8 us (98%)
  local copies, waits for them, and re-layouts  1.06 us (2%)
    pallas_call x1, Pallas kernels, on_device(): pl.pallas_call(kernel, out_shape=jax.ShapeDtypeStruct(adjoint.shape, F32)...  52.8 us

profile of v5, /device:TPU:1, one launch (start us, length us, event | category | flops | bytes accessed | tf_op | source)
XLA Modules:
  0.0 53.9 jit_solution(16680382232932693389)
XLA Ops:
  0.0 52.8 %shard_map.46 = f32[2,5,256,128]{3,2,1,0:T(8,128)S(1)} custom-call(s32[1,128]{1,0:T(1,128)} %bitcast.1, f32[2,5,256,128]{3,2,1,0:T(8,128)} %adj.1, f32[1,2,512,128]{3,2,1,0:T(8,128)} %fwd.1, bf16[10,256,256]{2,1,0:T(8,128)(2,1)} %constant.2.clone.consts), custom_call_target="tpu_custom_call" | custom-call | tf_op jit(solution)/shard_map/pallas_call | solution.py:410
  52.8 1.1 %copy.6 = f32[2,5,256,128]{3,2,1,0:T(8,128)} copy(f32[2,5,256,128]{3,2,1,0:T(8,128)S(1)} %shard_map.46) | data formatting | bytes 2621440
